TPU v7x, 32 devices: a whole 2x2x4 slice. The times are simulated.
32 devices in a mesh: dp: 8 (over y, x, core), mp: 4 (over z).
Axes of the slice: x: 2, y: 2, z: 4, core: 2. Of those that a mesh axis runs over, the one named last changes fastest.
Arguments:
- patches: bfloat16 [8192, 1024], P(('dp', 'mp')), as said below
- scene_ids: int32 [8192], P(('dp', 'mp')), may hold values from 0 to 7, as said below
- owner_ids: int32 [8192], P(('dp', 'mp')), may hold values from 0 to 7, as said below
- fill_slot: int32 [32768], P(('dp', 'mp')), may hold values from -1 to 511, as said below
- norm1_gain: float32 [1024], replicated, may hold values from 0.1 to 1.9
- norm1_bias: float32 [1024], replicated, may hold values from -1.75 to 1.75
- qkv_weight: bfloat16 [1024, 3, 1024], P(None, None, 'mp'), may hold values from -0.25 to 0.25
- qv_bias: float32 [2, 1024], P(None, 'mp'), may hold values from -3 to 3
- out_weight: bfloat16 [1024, 1024], P('mp'), may hold values from -1.5 to 1.5
- out_bias: float32 [1024], replicated, may hold values from -1.75 to 1.75
- norm2_gain: float32 [1024], replicated, may hold values from 0.1 to 1.9
- norm2_bias: float32 [1024], replicated, may hold values from -1.75 to 1.75
- up_weight: bfloat16 [1024, 4096], P(None, 'mp'), may hold values from -0.1875 to 0.1875
- up_bias: bfloat16 [4096], P('mp'), may hold values from -3 to 3
- down_weight: bfloat16 [4096, 1024], P('mp'), may hold values from -0.125 to 0.125
- down_bias: float32 [1024], replicated, may hold values from -1.75 to 1.75
- dec_weight: bfloat16 [1024, 512], replicated, may hold values from -0.1875 to 0.1875
- dec_bias: float32 [512], replicated, may hold values from -1.75 to 1.75
- mask_token: float32 [512], replicated, may hold values from -6 to 6
- positions: bfloat16 [32768, 512], P(('dp', 'mp')), may hold values from -6 to 6
- cotangent: bfloat16 [32768, 512], P(('dp', 'mp')), may hold values from -6 to 6
Outputs:
- decoder_in: bfloat16 [32768, 512], P(('dp', 'mp'))
- grad_patches: float32 [8192, 1024], P(('dp', 'mp'))
- grad_norm1_gain: float32 [1024], replicated
- grad_norm1_bias: float32 [1024], replicated
- grad_qkv_weight: float32 [1024, 3, 1024], P(None, None, 'mp')
- grad_qv_bias: float32 [2, 1024], P(None, 'mp')
- grad_out_weight: float32 [1024, 1024], P('mp')
- grad_out_bias: float32 [1024], replicated
- grad_norm2_gain: float32 [1024], replicated
- grad_norm2_bias: float32 [1024], replicated
- grad_up_weight: float32 [1024, 4096], P(None, 'mp')
- grad_up_bias: float32 [4096], P('mp')
- grad_down_weight: float32 [4096, 1024], P('mp')
- grad_down_bias: float32 [1024], replicated
- grad_dec_weight: float32 [1024, 512], replicated
- grad_dec_bias: float32 [512], replicated
- grad_mask_token: float32 [512], replicated
Inputs may be any that keep to these rules, and one draw needn't show every extreme that they name: `scene_ids`: within each group of 1024 rows (one dp index) scene ids start at 0 and rise by one at each scene boundary, never falling; scene 0 holds 256 to 512 rows, every other scene at least one. `owner_ids`: among the 256 rows of one device no owner is named more than 64 times; in each mp column one owner is named exactly 64 times by the rows of every device. `fill_slot`: in grid block e, slot s * 64 + r is named by exactly one cell when device (s, e % 4) has an r-th row (in row order) with owner e // 4, and by no cell otherwise. `patches`: magnitudes stay below 200.
All inputs are finite; a program needn't handle non-finite values.
Results may differ from a plain program's by a relative error of at most 0.013.
The roundings to bfloat16 on the way count: a program that leaves them out, or rounds other values in their place, can miss the bound.
Values may be sent and summed in bfloat16 or wider, within the bound.
A program may use at most 128 MiB of HBM per device.

v0:
```python
import jax
import jax.numpy as jnp
from jax import lax
from jax.sharding import PartitionSpec as P

HEAD_DIM = 64
QBLOCK = 512
NEG_FILL = -1000000000.0


def layer_norm(hidden, gain, bias_vec):
    centered = hidden - jnp.mean(hidden, axis=-1, keepdims=True)
    spread = jnp.mean(centered * centered, axis=-1, keepdims=True)
    return centered * lax.rsqrt(spread + 1e-06) * gain + bias_vec


def gelu_exact(values):
    return jax.nn.gelu(values, approximate=False)


def gather_rows(weight, data_par, model_par):
    rows, width = weight.shape
    part = rows // data_par
    mine = lax.dynamic_slice_in_dim(weight, lax.axis_index("dp") * part, part, 0)
    column = lax.all_gather(mine, "mp", axis=0)
    whole = lax.all_gather(column, "dp", axis=0)
    return whole.transpose(1, 0, 2, 3).reshape(model_par * rows, width)


def low(values):
    return values.astype(jnp.bfloat16)


def per_device(
    patches,
    scene_ids,
    owner_ids,
    fill_slot,
    norm1_gain,
    norm1_bias,
    qkv_weight,
    qv_bias,
    out_weight,
    out_bias,
    norm2_gain,
    norm2_bias,
    up_weight,
    up_bias,
    down_weight,
    down_bias,
    dec_weight,
    dec_bias,
    mask_token,
    positions,
    cotangent,
):
    row_count = patches.shape[0]
    model_par = lax.axis_size("mp")
    data_par = lax.axis_size("dp")
    group_rows = row_count * model_par
    total_rows = float(row_count * model_par * data_par)
    local_width = qkv_weight.shape[2]
    local_heads = local_width // HEAD_DIM
    score_scale = HEAD_DIM ** (-0.5)
    block_rows = min(QBLOCK, group_rows)
    block_starts = jnp.arange(group_rows // block_rows, dtype=jnp.int32) * block_rows
    capacity = 2 * row_count // data_par
    slot_count = capacity * data_par
    dec_width = dec_weight.shape[1]
    out_full = gather_rows(out_weight, data_par, model_par)
    inputs_f = patches.astype(jnp.float32)
    band_sums = lax.psum(
        (jnp.sum(inputs_f, axis=0), jnp.sum(inputs_f * inputs_f, axis=0)), ("dp", "mp")
    )
    band_mean = band_sums[0] / total_rows
    band_var = band_sums[1] / total_rows - band_mean * band_mean
    band_scale = lax.rsqrt(band_var + 1e-05)
    band_hat = (inputs_f - band_mean) * band_scale
    normed1 = layer_norm(band_hat, norm1_gain, norm1_bias).astype(jnp.bfloat16)
    norm1_all, scene_all = (
        lax.all_gather(normed1, "mp", axis=0, tiled=True),
        lax.all_gather(scene_ids, "mp", axis=0, tiled=True),
    )
    bias_three = jnp.stack([qv_bias[0], jnp.zeros_like(qv_bias[0]), qv_bias[1]])
    triples = (
        jnp.einsum("td,dcj->tcj", norm1_all, qkv_weight, preferred_element_type=jnp.float32)
        + bias_three
    ).astype(jnp.bfloat16)
    query_all = triples[:, 0].reshape(group_rows, local_heads, HEAD_DIM)
    key_all = triples[:, 1].reshape(group_rows, local_heads, HEAD_DIM)
    value_all = triples[:, 2].reshape(group_rows, local_heads, HEAD_DIM)

    def block_scores(first_row):
        query_blk = lax.dynamic_slice_in_dim(query_all, first_row, block_rows, 0)
        scene_blk = lax.dynamic_slice_in_dim(scene_all, first_row, block_rows, 0)
        scores = (
            jnp.einsum("qhd,khd->hqk", query_blk, key_all, preferred_element_type=jnp.float32)
            * score_scale
        )
        same_scene = (scene_blk[:, None] == scene_all[None, :])[None]
        return (jnp.where(same_scene, scores, NEG_FILL), query_blk)

    def attend_block(first_row):
        scores, query_blk = block_scores(first_row)
        row_max = jnp.max(scores, axis=-1, keepdims=True)
        exp_scores = jnp.exp(scores - row_max)
        row_total = jnp.sum(exp_scores, axis=-1, keepdims=True)
        softmax_w = (exp_scores / row_total).astype(jnp.bfloat16)
        mixed_rows = jnp.einsum(
            "hqk,khd->qhd", softmax_w, value_all, preferred_element_type=jnp.float32
        )
        return (mixed_rows.astype(jnp.bfloat16), (row_max + jnp.log(row_total))[..., 0])

    head_blocks, lse_blocks = lax.map(attend_block, block_starts)
    heads_out = head_blocks.reshape(group_rows, local_width)
    heads_rows = lax.all_to_all(heads_out, "mp", split_axis=0, concat_axis=1, tiled=True)
    attn_local = jnp.dot(heads_rows, out_full, preferred_element_type=jnp.float32)
    after_attn = band_hat + attn_local + out_bias
    normed2 = layer_norm(after_attn, norm2_gain, norm2_bias).astype(jnp.bfloat16)
    norm2_all = lax.all_gather(normed2, "mp", axis=0, tiled=True)
    pre_act = jnp.dot(norm2_all, up_weight, preferred_element_type=jnp.float32) + up_bias.astype(
        jnp.float32
    )
    act_rows = gelu_exact(pre_act).astype(jnp.bfloat16)
    mlp_part = low(jnp.dot(act_rows, down_weight, preferred_element_type=jnp.float32))
    proj_part = jnp.dot(mlp_part, dec_weight, preferred_element_type=jnp.float32)
    proj_sum = lax.psum_scatter(low(proj_part), "mp", scatter_dimension=0, tiled=True)
    direct = after_attn + down_bias
    projected = low(
        jnp.dot(low(direct), dec_weight, preferred_element_type=jnp.float32)
        + proj_sum.astype(jnp.float32)
        + dec_bias
    )
    owner_onehot = (owner_ids[:, None] == jnp.arange(data_par, dtype=jnp.int32)[None, :]).astype(
        jnp.int32
    )
    earlier = jnp.sum((jnp.cumsum(owner_onehot, axis=0) - owner_onehot) * owner_onehot, axis=1)
    send_slot = owner_ids * capacity + earlier
    slot_range = jnp.arange(slot_count, dtype=jnp.int32)
    send_onehot = (send_slot[:, None] == slot_range[None, :]).astype(jnp.bfloat16)
    outgoing = jnp.einsum(
        "rs,rc->sc", send_onehot, projected, preferred_element_type=jnp.float32
    ).astype(jnp.bfloat16)
    fill_onehot = (fill_slot[:, None] == slot_range[None, :]).astype(jnp.bfloat16)
    returning = jnp.einsum(
        "gs,gc->sc", fill_onehot, cotangent, preferred_element_type=jnp.float32
    ).astype(jnp.bfloat16)
    arrived, grad_back = (
        lax.all_to_all(
            outgoing.reshape(data_par, capacity, dec_width),
            "dp",
            split_axis=0,
            concat_axis=0,
            tiled=True,
        ),
        lax.all_to_all(
            returning.reshape(data_par, capacity, dec_width),
            "dp",
            split_axis=0,
            concat_axis=0,
            tiled=True,
        ),
    )
    placed = jnp.dot(
        fill_onehot, arrived.reshape(slot_count, dec_width), preferred_element_type=jnp.float32
    )
    masked = (fill_slot < 0)[:, None]
    decoder_in = (jnp.where(masked, mask_token, placed) + positions.astype(jnp.float32)).astype(
        jnp.bfloat16
    )
    grad_mask_local = jnp.sum(jnp.where(masked, cotangent.astype(jnp.float32), 0.0), axis=0)
    grad_proj = jnp.einsum(
        "rs,sc->rc",
        send_onehot,
        grad_back.reshape(slot_count, dec_width),
        preferred_element_type=jnp.float32,
    )
    grad_proj_low = grad_proj.astype(jnp.bfloat16)
    proj_grad_all = lax.all_gather(grad_proj_low, "mp", axis=0, tiled=True)
    grad_dec_local = jnp.einsum(
        "rd,rc->dc", low(direct), grad_proj_low, preferred_element_type=jnp.float32
    ) + jnp.einsum("rd,rc->dc", mlp_part, proj_grad_all, preferred_element_type=jnp.float32)
    grad_dec_bias_local = jnp.sum(grad_proj, axis=0)
    grad_block = jnp.einsum(
        "rc,dc->rd", grad_proj_low, dec_weight, preferred_element_type=jnp.float32
    )
    grad_down_bias_local = jnp.sum(low(grad_block).astype(jnp.float32), axis=0)
    grad_mlp_all = low(
        jnp.einsum("rc,dc->rd", proj_grad_all, dec_weight, preferred_element_type=jnp.float32)
    )
    grad_act = jnp.einsum(
        "tc,fc->tf", grad_mlp_all, down_weight, preferred_element_type=jnp.float32
    )
    grad_down_local = jnp.einsum(
        "tf,tc->fc", act_rows, grad_mlp_all, preferred_element_type=jnp.float32
    )
    down_sum = lax.psum(low(grad_down_local), "dp").astype(jnp.float32)
    gelu_val, gelu_back = jax.vjp(gelu_exact, pre_act)
    grad_pre = gelu_back(grad_act)[0].astype(jnp.bfloat16)
    grad_up_local = jnp.einsum("td,tf->df", norm2_all, grad_pre, preferred_element_type=jnp.float32)
    grad_up_bias_local = jnp.sum(grad_pre.astype(jnp.float32), axis=0)
    grad_norm2 = lax.psum_scatter(
        low(jnp.einsum("tf,df->td", grad_pre, up_weight, preferred_element_type=jnp.float32)),
        "mp",
        scatter_dimension=0,
        tiled=True,
    ).astype(jnp.float32)
    up_sum = lax.psum(low(grad_up_local), "dp").astype(jnp.float32)
    norm2_val, norm2_back = jax.vjp(layer_norm, after_attn, norm2_gain, norm2_bias)
    from_norm2, grad_gain2_local, grad_bias2_local = norm2_back(grad_norm2)
    grad_after = grad_block + from_norm2
    grad_attn = grad_after.astype(jnp.bfloat16)
    grad_out_bias_local = jnp.sum(grad_attn.astype(jnp.float32), axis=0)
    grad_out_rows = low(
        jnp.einsum("tj,tc->jc", heads_rows, grad_attn, preferred_element_type=jnp.float32)
    ).reshape(model_par, local_width, -1)
    out_part = lax.psum_scatter(grad_out_rows, "dp", scatter_dimension=1, tiled=True)
    out_part = lax.psum_scatter(out_part, "mp", scatter_dimension=0, tiled=True)
    out_sum = lax.all_gather(out_part[0], "dp", axis=0, tiled=True).astype(jnp.float32)
    grad_heads = lax.all_to_all(
        low(jnp.einsum("tc,jc->tj", grad_attn, out_full, preferred_element_type=jnp.float32)),
        "mp",
        split_axis=1,
        concat_axis=0,
        tiled=True,
    )
    grad_heads3 = grad_heads.reshape(group_rows, local_heads, HEAD_DIM)

    def back_block(carried, inputs):
        key_acc, value_acc = carried
        first_row, log_total = inputs
        scores, query_blk = block_scores(first_row)
        softmax_w = jnp.exp(scores - log_total[..., None])
        upstream = lax.dynamic_slice_in_dim(grad_heads3, first_row, block_rows, 0)
        value_acc = value_acc + jnp.einsum(
            "hqk,qhd->khd",
            softmax_w.astype(jnp.bfloat16),
            upstream,
            preferred_element_type=jnp.float32,
        )
        grad_probs = jnp.einsum(
            "qhd,khd->hqk", upstream, value_all, preferred_element_type=jnp.float32
        )
        inner_sum = jnp.sum(softmax_w * grad_probs, axis=-1, keepdims=True)
        grad_scores = (softmax_w * (grad_probs - inner_sum)).astype(jnp.bfloat16)
        grad_query = (
            jnp.einsum("hqk,khd->qhd", grad_scores, key_all, preferred_element_type=jnp.float32)
            * score_scale
        )
        key_acc = (
            key_acc
            + jnp.einsum("hqk,qhd->khd", grad_scores, query_blk, preferred_element_type=jnp.float32)
            * score_scale
        )
        return ((key_acc, value_acc), grad_query.astype(jnp.bfloat16))

    zero_heads = jnp.zeros((group_rows, local_heads, HEAD_DIM), jnp.float32)
    (key_grad, value_grad), query_blocks = lax.scan(
        back_block, (zero_heads, zero_heads), (block_starts, lse_blocks)
    )
    grad_triples = jnp.stack(
        [
            query_blocks.reshape(group_rows, local_width),
            key_grad.reshape(group_rows, local_width).astype(jnp.bfloat16),
            value_grad.reshape(group_rows, local_width).astype(jnp.bfloat16),
        ],
        axis=1,
    )
    grad_qkv_local = jnp.einsum(
        "td,tcj->dcj", norm1_all, grad_triples, preferred_element_type=jnp.float32
    )
    triple_sums = jnp.sum(grad_triples.astype(jnp.float32), axis=0)
    grad_qv_local = jnp.stack([triple_sums[0], triple_sums[2]])
    grad_norm1 = lax.psum_scatter(
        low(
            jnp.einsum("tcj,dcj->td", grad_triples, qkv_weight, preferred_element_type=jnp.float32)
        ),
        "mp",
        scatter_dimension=0,
        tiled=True,
    ).astype(jnp.float32)
    qkv_sum = lax.psum(low(grad_qkv_local), "dp").astype(jnp.float32)
    norm1_val, norm1_back = jax.vjp(layer_norm, band_hat, norm1_gain, norm1_bias)
    from_norm1, grad_gain1_local, grad_bias1_local = norm1_back(grad_norm1)
    grad_hat = grad_after + from_norm1
    dec_sum = lax.psum(low(grad_dec_local), ("dp", "mp")).astype(jnp.float32)
    summed_small = lax.psum((grad_qv_local, grad_up_bias_local), "dp")
    shared = lax.psum(
        (
            jnp.sum(grad_hat, axis=0),
            jnp.sum(grad_hat * band_hat, axis=0),
            grad_gain1_local,
            grad_bias1_local,
            grad_gain2_local,
            grad_bias2_local,
            grad_out_bias_local,
            grad_down_bias_local,
            grad_dec_bias_local,
            grad_mask_local,
        ),
        ("dp", "mp"),
    )
    grad_patches = band_scale * (
        grad_hat - shared[0] / total_rows - band_hat * (shared[1] / total_rows)
    )
    return (
        decoder_in,
        grad_patches,
        shared[2],
        shared[3],
        qkv_sum,
        summed_small[0],
        out_sum,
        shared[6],
        shared[4],
        shared[5],
        up_sum,
        summed_small[1],
        down_sum,
        shared[7],
        dec_sum,
        shared[8],
        shared[9],
    )


def solution(mesh):
    in_specs = (
        P(("dp", "mp"), None),
        P(("dp", "mp")),
        P(("dp", "mp")),
        P(("dp", "mp")),
        P(),
        P(),
        P(None, None, "mp"),
        P(None, "mp"),
        P("mp", None),
        P(),
        P(),
        P(),
        P(None, "mp"),
        P("mp"),
        P("mp", None),
        P(),
        P(),
        P(),
        P(),
        P(("dp", "mp"), None),
        P(("dp", "mp"), None),
    )
    out_specs = (
        P(("dp", "mp"), None),
        P(("dp", "mp"), None),
        P(),
        P(),
        P(None, None, "mp"),
        P(None, "mp"),
        P("mp", None),
        P(),
        P(),
        P(),
        P(None, "mp"),
        P("mp"),
        P("mp", None),
        P(),
        P(),
        P(),
        P(),
    )
    return jax.shard_map(
        per_device, mesh=mesh, in_specs=in_specs, out_specs=out_specs, check_vma=False
    )
```

profile of v0, /device:TPU:0, one launch (start us, length us, event | category | flops | bytes accessed | tf_op | source)
XLA Modules:
  0.0 733.2 jit_solution(15494136100213632518)
XLA Ops:
  8.6 42.1 %all-reduce.1 = (f32[1024]{0:T(1024)S(1)}, f32[1024]{0:T(1024)S(1)}) all-reduce(f32[1024]{0:T(1024)S(1)} %get-tuple-element.181, f32[1024]{0:T(1024)S(1)} %get-tuple-element.180), channel_id=1, replica_groups=mesh['dp'=8,'mp'=4] {'dp','mp'}, use_global_device_ids=true, to_apply=%region_6.7 | all-reduce | flops 2048 | bytes 16384 | tf_op jit(solution)/shard_map/psum | solution.py:72
  63.7 17.0 %all-gather = bf16[128,1024]{1,0:T(8,128)(2,1)} all-gather(bf16[32,1024]{1,0:T(8,128)(2,1)S(1)} %constant_dynamic-slice_fusion), channel_id=2, replica_groups=mesh['dp'=8,'mp'=4] {'mp'}, dimensions={0}, use_global_device_ids=true | all-gather | bytes 327680 | tf_op jit(solution)/shard_map/all_gather | solution.py:25
  80.8 10.5 %all-gather.3 = s32[4,1,256]{2,1,0:T(1,128)S(1)} all-gather(s32[1,1,256]{2,1,0:T(1,128)S(1)} %bitcast.166), channel_id=1, replica_groups=mesh['dp'=8,'mp'=4] {'mp'}, dimensions={0}, use_global_device_ids=true | all-gather | bytes 5120 | tf_op jit(solution)/shard_map/all_gather | solution.py:82
  92.4 13.1 %all-gather.9.cloned.1.call-done = bf16[1024,1024]{1,0:T(8,128)(2,1)} async-done(((bf16[256,1024]{1,0:T(8,128)(2,1)}), bf16[1024,1024]{1,0:T(8,128)(2,1)}) %all-gather.9.cloned.1.call-update) | async-done | bytes 2097168 | tf_op jit(solution)/shard_map/all_gather | solution.py:81
  111.2 22.3 %while.27 = (s32[]{:T(128)}, bf16[2,512,4,64]{1,3,2,0:T(8,128)(2,1)}, f32[2,4,512]{2,1,0:T(4,128)S(1)}, s32[2]{0:T(128)S(1)}, s32[1024]{0:T(1024)S(1)}, /*index=...) while((s32[]{:T(128)}, ...), condition=%wide.region_12.13_spmd, body=%wide.region_9.12_spmd.sunk | while | flops 562690048 | bytes 35203332 | solution.py:114
  151.9 8.4 %all-to-all-done = bf16[4,256,256]{1,2,0:T(8,128)(2,1)} async-done(((bf16[4,256,256]{1,2,0:T(8,128)(2,1)}), bf16[4,256,256]{1,2,0:T(8,128)(2,1)}, u32[]{:S(2)}, u32[]{:S(2)}) %all-to-all-start) | async-done | bytes 524320 | tf_op jit(solution)/shard_map/all_to_all | solution.py:116
  165.1 13.0 %all-gather.13.cloned.1.call-done = bf16[1024,512]{1,0:T(8,128)(2,1)} async-done(((bf16[256,512]{1,0:T(8,128)(2,1)}), bf16[1024,512]{1,0:T(8,128)(2,1)}) %all-gather.13.cloned.1.call-update) | async-done | bytes 1048592 | tf_op jit(solution)/shard_map/all_gather | solution.py:179
  182.2 42.9 %all-gather.11.cloned.1.call-done = bf16[1024,1024]{1,0:T(8,128)(2,1)} async-done(((bf16[256,1024]{1,0:T(8,128)(2,1)}), bf16[1024,1024]{1,0:T(8,128)(2,1)}) %all-gather.11.cloned.1.call-update) | async-done | bytes 2097168 | tf_op jit(solution)/shard_map/all_gather | solution.py:120
  225.1 4.7 fusion.106
  229.9 13.9 %convert_reduce_fusion = (f32[1024]{0:T(1024)}, bf16[1024,1024]{1,0:T(8,128)(2,1)S(1)}, f32[1024,1024]{1,0:T(8,128)}) fusion(f32[1024,1024]{1,0:T(8,128)S(1)} %fusion.106, f32[1024]{0:T(1024)S(1)} %convert_element_type.184, bf16[1024,1024]{1,0:T(8,128)(2,1)S(1)} %copy-done.61, bf16[1024,1024]{1,0:T(8,128)(2,1)S(1)} %copy-done), kind=kOutput, calls=%fused_computation.48 | convolution fusion | flops 2226125824 | bytes 14688256 | tf_op jit(solution)/shard_map/tc,fc->tf/dot_general | solution.py:191
  248.9 42.5 %reduce-scatter.8.cloned.1.call-done = bf16[256,1024]{1,0:T(8,128)(2,1)} async-done(((bf16[1024,1024]{1,0:T(8,128)(2,1)}), bf16[256,1024]{1,0:T(8,128)(2,1)}) %reduce-scatter.8.cloned.1.call-update) | async-done | bytes 524304 | tf_op jit(solution)/shard_map/reduce_scatter | solution.py:202
  302.1 4.6 multiply_convert_fusion.1
  329.2 6.1 convolution_convert_fusion.1
  335.3 5.1 all-to-all-done.3
  343.7 30.6 %while.28 = (s32[]{:T(128)}, f32[1024,4,64]{0,2,1:T(8,128)S(1)}, f32[1024,4,64]{0,2,1:T(8,128)}, bf16[2,512,4,64]{1,3,2,0:T(8,128)(2,1)}, s32[2]{0:T(128)S(1)}, ...) while((s32[]{:T(128)}, f32[1024,4,64]{0,2,1:T(8,128)S(1)}, ...), condition=%wide.region_21.22_spmd.clone, body=%wide.region_19.21_spmd.clone.sunk | while | flops 1375729664 | bytes 84740432 | solution.py:258
  378.6 4.6 fusion.50
  383.9 4.6 bitcast_convert_fusion
  396.6 110.9 %all-reduce.7.cloned.1.call-done = bf16[1024,512]{1,0:T(8,128)(2,1)} async-done(((bf16[1024,512]{1,0:T(8,128)(2,1)}), bf16[1024,512]{1,0:T(8,128)(2,1)}) %all-reduce.7.cloned.1.call-update) | async-done | bytes 1048592 | tf_op jit(solution)/shard_map/psum | solution.py:286
  513.7 13.4 %all-reduce.2 = (f32[2,256]{1,0:T(2,128)}, f32[1024]{0:T(1024)}) all-reduce(f32[2,256]{1,0:T(2,128)S(1)} %pad_maximum_fusion.2, f32[1024]{0:T(1024)S(1)} %copy-done.49), channel_id=1, replica_groups=mesh['dp'=8,'mp'=4] {'dp'}, use_global_device_ids=true, to_apply=%region_35.36 | all-reduce | flops 1536 | bytes 12288 | tf_op jit(solution)/shard_map/psum | solution.py:287
  527.1 82.7 %all-reduce.9.cloned.1.call-done = (bf16[1024,3,256]{2,0,1:T(8,128)(2,1)}, bf16[1024,1024]{1,0:T(8,128)(2,1)}, bf16[1024,1024]{1,0:T(8,128)(2,1)}) async-done(((bf16[1024,3,256]{2,0,1:T(8,128)(2,1)}, bf16[1024,1024]{1,0:T(8,128)(2,1)}, bf16[1024,1024]{1,0:T(8,128)(2,1)}), (bf16[1024,3,256]{2,0,1:T(8,128)(2,1)}, bf16[1024,1024]{1,0:T(8,128)(2,1)}, bf16[1024,1024]{1,0:T(8,128)(2,1)})) %all-reduce.9.cloned.1.call-update) | async-done | bytes 5767184 | tf_op jit(solution)/shard_map/psum | solution.py:282
  618.4 13.7 %reduce-scatter.14.cloned.1.call-done = bf16[1,32,1024]{2,1,0:T(8,128)(2,1)} async-done(((bf16[4,32,1024]{2,1,0:T(8,128)(2,1)}), bf16[1,32,1024]{2,1,0:T(8,128)(2,1)}) %reduce-scatter.14.cloned.1.call-update) | async-done | bytes 65552 | tf_op jit(solution)/shard_map/reduce_scatter | solution.py:218
  632.1 10.1 %all-gather.2 = bf16[1,256,1024]{2,1,0:T(8,128)(2,1)S(1)} all-gather(bf16[1,32,1024]{2,1,0:T(8,128)(2,1)} %reduce-scatter.14.cloned.1.call-done), channel_id=4, replica_groups=mesh['dp'=8,'mp'=4] {'dp'}, dimensions={1}, use_global_device_ids=true | all-gather | bytes 589824 | tf_op jit(solution)/shard_map/all_gather | solution.py:219
  643.2 33.0 %reduce-scatter.10.cloned.1.call-done = bf16[256,1024]{1,0:T(8,128)(2,1)} async-done(((bf16[1024,1024]{1,0:T(8,128)(2,1)}), bf16[256,1024]{1,0:T(8,128)(2,1)}) %reduce-scatter.10.cloned.1.call-update) | async-done | bytes 524304 | tf_op jit(solution)/shard_map/reduce_scatter | solution.py:274
  683.4 40.7 %all-reduce = (f32[1024]{0:T(1024)S(1)}, f32[1024]{0:T(1024)S(1)}, f32[1024]{0:T(1024)}, f32[1024]{0:T(1024)}, f32[1024]{0:T(1024)}, /*index=5*/f32[1024]{0:T(10...) all-reduce(f32[1024]{0:T(1024)S(1)} %get-tuple-element.176, ...), channel_id=1, replica_groups=mesh['dp'=8,'mp'=4] {'dp','mp'}, use_global_device_ids=true, to_apply=%region_28.29 | all-reduce | flops 9216 | bytes 73728 | tf_op jit(solution)/shard_map/psum | solution.py:288
  (287 shorter events, 172.3 us)
Async XLA Ops:
  7.2 222.6 %copy-start = (bf16[1024,1024]{1,0:T(8,128)(2,1)S(1)}, bf16[1024,1024]{1,0:T(8,128)(2,1)}, u32[]{:S(2)}) copy-start(bf16[1024,1024]{1,0:T(8,128)(2,1)} %param.39) | copy-start | bytes 6291460
  7.2 73.6 %copy-start.52 = (f32[2,256]{1,0:T(2,128)S(1)}, f32[2,256]{1,0:T(2,128)}, u32[]{:S(2)}) copy-start(f32[2,256]{1,0:T(2,128)} %param.32) | copy-start | bytes 6148
  7.2 73.6 %copy-start.53 = (s32[256]{0:T(256)S(1)}, s32[256]{0:T(256)}, u32[]{:S(2)}) copy-start(s32[256]{0:T(256)} %param.26) | copy-start | bytes 3076
  7.2 84.1 %copy-start.43 = (s32[256]{0:T(256)S(1)}, s32[256]{0:T(256)}, u32[]{:S(2)}) copy-start(s32[256]{0:T(256)} %param.27) | copy-start | bytes 3076
  7.2 98.2 %all-gather.9.cloned.1.call-start = ((), (), s32[]{:S(2)}) async-start(), calls=%async_computation.9 | async-start | bytes 2621440 | tf_op jit(solution)/shard_map/all_gather | solution.py:81
  50.7 109.6 %copy-start.27 = (f32[1024]{0:T(1024)}, f32[1024]{0:T(1024)S(1)}, u32[]{:S(2)}) copy-start(f32[1024]{0:T(1024)S(1)} %get-tuple-element.257) | copy-start | bytes 12292
  50.7 109.6 %copy-start.29 = (f32[1024]{0:T(1024)}, f32[1024]{0:T(1024)S(1)}, u32[]{:S(2)}) copy-start(f32[1024]{0:T(1024)S(1)} %get-tuple-element.258) | copy-start | bytes 12292
  58.6 82.9 %all-to-all-start.2 = ((bf16[8,64,512]{2,1,0:T(8,128)(2,1)}), bf16[8,64,512]{2,1,0:T(8,128)(2,1)}, u32[]{:S(2)}, u32[]{:S(2)}) async-start(bf16[8,64,512]{2,1,0:T(8,128)(2,1)} %bitcast.21), calls=%async_computation.3 | async-start | bytes 1048576 | tf_op jit(solution)/shard_map/all_to_all | solution.py:156
  62.8 85.9 %all-gather.15.cloned.1.call-start = ((), (), s32[]{:S(2)}) async-start(), calls=%async_computation.18 | async-start | bytes 2359296 | tf_op jit(solution)/shard_map/all_gather | solution.py:26
  141.5 18.8 %all-to-all-start = ((bf16[4,256,256]{1,2,0:T(8,128)(2,1)}), bf16[4,256,256]{1,2,0:T(8,128)(2,1)}, u32[]{:S(2)}, u32[]{:S(2)}) async-start(bf16[4,256,256]{1,2,0:T(8,128)(2,1)} %copy.76), calls=%async_computation | async-start | bytes 1048576 | tf_op jit(solution)/shard_map/all_to_all | solution.py:116
  145.7 32.4 %all-gather.13.cloned.1.call-start = ((), (), s32[]{:S(2)}) async-start(), calls=%async_computation.12 | async-start | bytes 1310720 | tf_op jit(solution)/shard_map/all_gather | solution.py:179
  148.6 76.5 %all-gather.11.cloned.1.call-start = ((), (), s32[]{:S(2)}) async-start(), calls=%async_computation.10 | async-start | bytes 2621440 | tf_op jit(solution)/shard_map/all_gather | solution.py:120
  165.0 126.5 %reduce-scatter.8.cloned.1.call-start = ((), (), s32[]{:S(2)}) async-start(), calls=%async_computation.13 | async-start | bytes 2621440 | tf_op jit(solution)/shard_map/reduce_scatter | solution.py:202
  248.9 134.4 %reduce-scatter.12.cloned.1.call-start = ((), (), s32[]{:S(2)}) async-start(), calls=%async_computation.15 | async-start | bytes 2359296 | tf_op jit(solution)/shard_map/reduce_scatter | solution.py:217
  301.9 86.7 %reduce-scatter.6.cloned.1.call-start = ((), (), s32[]{:S(2)}) async-start(), calls=%async_computation.11 | async-start | bytes 1310720 | tf_op jit(solution)/shard_map/reduce_scatter | solution.py:127
  322.5 17.9 %all-to-all-start.3 = ((bf16[256,4,256]{2,0,1:T(8,128)(2,1)}), bf16[256,4,256]{2,0,1:T(8,128)(2,1)S(1)}, u32[]{:S(2)}, u32[]{:S(2)}) async-start(bf16[256,4,256]{2,0,1:T(8,128)(2,1)} %bitcast.160), calls=%async_computation.5 | async-start | bytes 1048576 | tf_op jit(solution)/shard_map/all_to_all | solution.py:220
  326.0 181.6 %all-reduce.7.cloned.1.call-start = ((), (), s32[]{:S(2)}) async-start(), calls=%async_computation.17 | async-start | bytes 2097152 | tf_op jit(solution)/shard_map/psum | solution.py:286
  329.2 280.7 %all-reduce.9.cloned.1.call-start = ((), (), s32[]{:S(2)}) async-start(), calls=%async_computation.19 | async-start | bytes 11534336 | tf_op jit(solution)/shard_map/psum | solution.py:282
  383.2 248.9 %reduce-scatter.14.cloned.1.call-start = ((), (), s32[]{:S(2)}) async-start(), calls=%async_computation.16 | async-start | bytes 327680 | tf_op jit(solution)/shard_map/reduce_scatter | solution.py:218
  383.8 292.4 %reduce-scatter.10.cloned.1.call-start = ((), (), s32[]{:S(2)}) async-start(), calls=%async_computation.14 | async-start | bytes 2621440 | tf_op jit(solution)/shard_map/reduce_scatter | solution.py:274
  388.5 121.8 %copy-start.59 = (f32[512]{0:T(512)S(1)}, f32[512]{0:T(512)}, u32[]{:S(2)}) copy-start(f32[512]{0:T(512)} %param.43) | copy-start | bytes 6148
  391.4 119.0 %all-to-all-start.1 = ((bf16[8,64,512]{2,1,0:T(8,128)(2,1)}), bf16[8,64,512]{2,1,0:T(8,128)(2,1)S(1)}, u32[]{:S(2)}, u32[]{:S(2)}) async-start(bf16[8,64,512]{2,1,0:T(8,128)(2,1)} %bitcast.19), calls=%async_computation.2 | async-start | bytes 1048576 | tf_op jit(solution)/shard_map/all_to_all | solution.py:149
  396.6 117.2 %copy-start.49 = (f32[1024]{0:T(1024)S(1)}, f32[1024]{0:T(1024)}, u32[]{:S(2)}) copy-start(f32[1024]{0:T(1024)} %get-tuple-element.237) | copy-start | bytes 12292
  618.4 65.0 %copy-start.51 = (f32[512]{0:T(512)S(1)}, f32[512]{0:T(512)}, u32[]{:S(2)}) copy-start(f32[512]{0:T(512)} %get-tuple-element.253) | copy-start | bytes 6148
  (62 other events, 1068.7 us)
Sparse Core Ops, SparseCore 0:
  55.7 49.7 all-gather.8
  107.4 26.6 all-gather.14
  148.7 29.2 all-gather.12
  180.1 45.0 all-gather.10
  249.0 42.4 reduce-scatter.7
  302.0 40.2 reduce-scatter.11
  345.2 27.3 reduce-scatter.5
  378.3 129.2 all-reduce.6
  512.3 97.5 all-reduce.8
  612.0 20.0 reduce-scatter.13
  634.4 41.8 reduce-scatter.9
where the time goes:
time: 743 us; the launch traced here: 733 us
  waiting for transfers between devices  366 us (49%)
  blocking collectives  134 us (18%)
  matrix products  111 us (15%)
  other arithmetic  52.9 us (7%)
  local copies, waits for them, and re-layouts  30 us (4%)
  starting transfers between devices  16.3 us (2%)
  between operations  14.9 us (2%)
  loops' own time  8.35 us (1%)
    psum x1, waiting for transfers between devices, per_device(): dec_sum = lax.psum(low(grad_dec_local), ('dp', 'mp')).astype(jnp.float32)  111 us
    psum x1, waiting for transfers between devices, per_device(): qkv_sum = lax.psum(low(grad_qkv_local), 'dp').astype(jnp.float32)  82.7 us
    all_gather x1, waiting for transfers between devices, per_device(): norm2_all = lax.all_gather(normed2, 'mp', axis=0, tiled=True)  42.9 us
    reduce_scatter x1, waiting for transfers between devices, per_device(): lax.psum_scatter(low(jnp.einsum('tf,df->td', grad_pre, up_weight, preferr...  42.5 us
    psum x1, blocking collectives, per_device(): lax.psum((jnp.sum(inputs_f, axis=0), jnp.sum(inputs_f * inputs_f, axis=0)...  42.1 us
    psum x1, blocking collectives, per_device(): lax.psum((jnp.sum(grad_hat, axis=0), jnp.sum(grad_hat * band_hat, axis=0)...  40.7 us
    reduce_scatter x1, waiting for transfers between devices, per_device(): lax.psum_scatter(low(jnp.einsum('tcj,dcj->td', grad_triples, qkv_weight,...  33 us
    all_gather x1, blocking collectives, gather_rows(): column = lax.all_gather(mine, 'mp', axis=0)  17 us
  transfers between devices with their start and end apart: 15, of which 10 were waited for; matrix products, arithmetic and copies ran while one was open for 19% of the time, Pallas kernels for 0%

commit v1 on v0

--- a/solution.py
+++ b/solution.py
@@ -6,6 +6,27 @@
 HEAD_DIM = 64
 QBLOCK = 512
 NEG_FILL = -1000000000.0
+
+
+def in_order(blocks, dim):
+    blocks = jnp.moveaxis(blocks, 0, dim)
+    lengths = blocks.shape
+    return blocks.reshape(*lengths[:dim], lengths[dim] * lengths[dim + 1], *lengths[dim + 2 :])
+
+
+def doubled(x, axis):
+    length, here = (lax.axis_size(axis), lax.axis_index(axis))
+    parts, stride = (x[None], 1)
+    while stride < length:
+        other = lax.ppermute(parts, axis, [(i, i ^ stride) for i in range(length)])
+        low = here & stride == 0
+        parts = jnp.concatenate([jnp.where(low, parts, other), jnp.where(low, other, parts)])
+        stride *= 2
+    return parts
+
+
+def doubled_up(shard, axis, dim):
+    return in_order(doubled(shard, axis), dim)
 
 
 def layer_norm(hidden, gain, bias_vec):
@@ -117,7 +138,7 @@
     attn_local = jnp.dot(heads_rows, out_full, preferred_element_type=jnp.float32)
     after_attn = band_hat + attn_local + out_bias
     normed2 = layer_norm(after_attn, norm2_gain, norm2_bias).astype(jnp.bfloat16)
-    norm2_all = lax.all_gather(normed2, "mp", axis=0, tiled=True)
+    norm2_all = doubled_up(normed2, "mp", 0)
     pre_act = jnp.dot(norm2_all, up_weight, preferred_element_type=jnp.float32) + up_bias.astype(
         jnp.float32
     )

time: 743 us -> 762 us (1.026)
  waiting for transfers between devices: 366 us -> 384 us
    all_gather x1 -> x0, waiting for transfers between devices: 42.9 us -> none  [per_device(): norm2_all = lax.all_gather(normed2, 'mp', axis=0, tiled=True)]
    all_gather x1, waiting for transfers between devices: 13 us -> 44.5 us  [per_device(): proj_grad_all = lax.all_gather(grad_proj_low, 'mp', axis=0, tiled=True)]
    ppermute x0 -> x2, waiting for transfers between devices: none -> 19.1 us  [doubled(): other = lax.ppermute(parts, axis, [(i, i ^ stride) for i in range(length)])]
  transfers between devices with their start and end apart: 15 -> 16, of which waited for: 10 -> 12; matrix products, arithmetic and copies ran while one was open for 19% -> 18% of each run, Pallas kernels for 0% -> 0%
where the time goes in v1:
time: 762 us; the launch traced here: 752 us
  waiting for transfers between devices  384 us (50%)
  blocking collectives  133 us (17%)
  matrix products  107 us (14%)
  other arithmetic  56.5 us (7%)
  local copies, waits for them, and re-layouts  30.9 us (4%)
  starting transfers between devices  16.6 us (2%)
  between operations  15.2 us (2%)
  loops' own time  8.07 us (1%)
    psum x1, waiting for transfers between devices, per_device(): dec_sum = lax.psum(low(grad_dec_local), ('dp', 'mp')).astype(jnp.float32)  111 us
    psum x1, waiting for transfers between devices, per_device(): qkv_sum = lax.psum(low(grad_qkv_local), 'dp').astype(jnp.float32)  82.7 us
    all_gather x1, waiting for transfers between devices, per_device(): proj_grad_all = lax.all_gather(grad_proj_low, 'mp', axis=0, tiled=True)  44.5 us
    reduce_scatter x1, waiting for transfers between devices, per_device(): lax.psum_scatter(low(jnp.einsum('tf,df->td', grad_pre, up_weight, preferr...  42.6 us
    psum x1, blocking collectives, per_device(): lax.psum((jnp.sum(inputs_f, axis=0), jnp.sum(inputs_f * inputs_f, axis=0)...  42.1 us
    psum x1, blocking collectives, per_device(): lax.psum((jnp.sum(grad_hat, axis=0), jnp.sum(grad_hat * band_hat, axis=0)...  40.7 us
    reduce_scatter x1, waiting for transfers between devices, per_device(): lax.psum_scatter(low(jnp.einsum('tcj,dcj->td', grad_triples, qkv_weight,...  32.9 us
    ppermute x2, waiting for transfers between devices, doubled(): other = lax.ppermute(parts, axis, [(i, i ^ stride) for i in range(length)])  19.1 us
  transfers between devices with their start and end apart: 16, of which 12 were waited for; matrix products, arithmetic and copies ran while one was open for 18% of the time, Pallas kernels for 0%

profile of v1, /device:TPU:0, one launch (start us, length us, event | category | flops | bytes accessed | tf_op | source)
XLA Modules:
  0.0 751.7 jit_solution(10242478951210121632)
XLA Ops:
  8.6 42.1 %all-reduce.1 = (f32[1024]{0:T(1024)S(1)}, f32[1024]{0:T(1024)S(1)}) all-reduce(f32[1024]{0:T(1024)S(1)} %get-tuple-element.181, f32[1024]{0:T(1024)S(1)} %get-tuple-element.180), channel_id=1, replica_groups=mesh['dp'=8,'mp'=4] {'dp','mp'}, use_global_device_ids=true, to_apply=%region_6.7 | all-reduce | flops 2048 | bytes 16384 | tf_op jit(solution)/shard_map/psum | solution.py:93
  56.5 16.7 %all-gather = bf16[128,1024]{1,0:T(8,128)(2,1)} all-gather(bf16[32,1024]{1,0:T(8,128)(2,1)S(1)} %constant_dynamic-slice_fusion), channel_id=2, replica_groups=mesh['dp'=8,'mp'=4] {'mp'}, dimensions={0}, use_global_device_ids=true | all-gather | bytes 327680 | tf_op jit(solution)/shard_map/all_gather | solution.py:46
  74.0 10.0 %all-gather.3 = s32[4,1,256]{2,1,0:T(1,128)S(1)} all-gather(s32[1,1,256]{2,1,0:T(1,128)} %bitcast.174), channel_id=1, replica_groups=mesh['dp'=8,'mp'=4] {'mp'}, dimensions={0}, use_global_device_ids=true | all-gather | bytes 5120 | tf_op jit(solution)/shard_map/all_gather | solution.py:103
  84.2 18.6 %all-gather.8.cloned.1.call-done = bf16[1024,1024]{1,0:T(8,128)(2,1)} async-done(((bf16[256,1024]{1,0:T(8,128)(2,1)}), bf16[1024,1024]{1,0:T(8,128)(2,1)}) %all-gather.8.cloned.1.call-update) | async-done | bytes 2097168 | tf_op jit(solution)/shard_map/all_gather | solution.py:102
  108.4 22.3 %while.27 = (s32[]{:T(128)}, bf16[2,512,4,64]{1,3,2,0:T(8,128)(2,1)}, f32[2,4,512]{2,1,0:T(4,128)S(1)}, s32[2]{0:T(128)S(1)}, s32[1024]{0:T(1024)S(1)}, /*index=...) while((s32[]{:T(128)}, ...), condition=%wide.region_12.13_spmd, body=%wide.region_9.12_spmd.sunk | while | flops 562690048 | bytes 35203332 | solution.py:135
  149.6 7.6 %all-to-all-done = bf16[4,256,256]{1,2,0:T(8,128)(2,1)} async-done(((bf16[4,256,256]{1,2,0:T(8,128)(2,1)}), bf16[4,256,256]{1,2,0:T(8,128)(2,1)}, u32[]{:S(2)}, u32[]{:S(2)}) %all-to-all-start) | async-done | bytes 524320 | tf_op jit(solution)/shard_map/all_to_all | solution.py:137
  165.5 5.5 all-to-all-done.2
  173.8 6.0 collective-permute-done
  183.7 44.5 %all-gather.10.cloned.1.call-done = bf16[1024,512]{1,0:T(8,128)(2,1)} async-done(((bf16[256,512]{1,0:T(8,128)(2,1)}), bf16[1024,512]{1,0:T(8,128)(2,1)}) %all-gather.10.cloned.1.call-update) | async-done | bytes 1048592 | tf_op jit(solution)/shard_map/all_gather | solution.py:200
  231.1 13.1 %collective-permute-done.1 = bf16[2,256,1024]{2,1,0:T(8,128)(2,1)} collective-permute-done((bf16[2,256,1024]{2,1,0:T(8,128)(2,1)}, bf16[2,256,1024]{2,1,0:T(8,128)(2,1)}, u32[]{:S(2)}, u32[]{:S(2)}) %collective-permute-start.1) | collective-permute-done | bytes 1048608 | tf_op jit(solution)/shard_map/ppermute | solution.py:21
  248.2 13.9 %convert_reduce_fusion = (f32[1024]{0:T(1024)}, bf16[1024,1024]{1,0:T(8,128)(2,1)S(1)}, f32[1024,1024]{1,0:T(8,128)}) fusion(f32[1024,1024]{1,0:T(8,128)S(1)} %fusion.107, f32[1024]{0:T(1024)S(1)} %convert_element_type.184, bf16[1024,1024]{1,0:T(8,128)(2,1)S(1)} %convolution_convert_fusion.4, bf16[1024,1024]{1,0:T(8,128)(2,1)S(1)} %copy-done), kind=kOutput, calls=%fused_computation.48 | convolution fusion | flops 2226125824 | bytes 14688256 | tf_op jit(solution)/shard_map/tc,fc->tf/dot_general | solution.py:212
  267.3 42.6 %reduce-scatter.8.cloned.1.call-done = bf16[256,1024]{1,0:T(8,128)(2,1)} async-done(((bf16[1024,1024]{1,0:T(8,128)(2,1)}), bf16[256,1024]{1,0:T(8,128)(2,1)}) %reduce-scatter.8.cloned.1.call-update) | async-done | bytes 524304 | tf_op jit(solution)/shard_map/reduce_scatter | solution.py:223
  347.6 6.1 convolution_convert_fusion
  353.7 5.1 all-to-all-done.3
  362.1 30.3 %while.28 = (s32[]{:T(128)}, f32[1024,4,64]{0,2,1:T(8,128)S(1)}, f32[1024,4,64]{0,2,1:T(8,128)}, bf16[2,512,4,64]{1,3,2,0:T(8,128)(2,1)}, s32[2]{0:T(128)S(1)}, ...) while((s32[]{:T(128)}, f32[1024,4,64]{0,2,1:T(8,128)S(1)}, ...), condition=%wide.region_21.22_spmd.clone, body=%wide.region_19.21_spmd.clone.sunk | while | flops 1375729664 | bytes 84740432 | solution.py:279
  396.7 4.6 fusion.50
  402.1 4.6 bitcast_convert_fusion
  414.9 110.9 %all-reduce.7.cloned.1.call-done = bf16[1024,512]{1,0:T(8,128)(2,1)} async-done(((bf16[1024,512]{1,0:T(8,128)(2,1)}), bf16[1024,512]{1,0:T(8,128)(2,1)}) %all-reduce.7.cloned.1.call-update) | async-done | bytes 1048592 | tf_op jit(solution)/shard_map/psum | solution.py:307
  531.9 13.4 %all-reduce.2 = (f32[2,256]{1,0:T(2,128)}, f32[1024]{0:T(1024)}) all-reduce(f32[2,256]{1,0:T(2,128)S(1)} %pad_maximum_fusion.4, f32[1024]{0:T(1024)S(1)} %copy-done.53), channel_id=1, replica_groups=mesh['dp'=8,'mp'=4] {'dp'}, use_global_device_ids=true, to_apply=%region_35.36 | all-reduce | flops 1536 | bytes 12288 | tf_op jit(solution)/shard_map/psum | solution.py:308
  545.3 82.7 %all-reduce.9.cloned.1.call-done = (bf16[1024,3,256]{2,0,1:T(8,128)(2,1)}, bf16[1024,1024]{1,0:T(8,128)(2,1)}, bf16[1024,1024]{1,0:T(8,128)(2,1)}) async-done(((bf16[1024,3,256]{2,0,1:T(8,128)(2,1)}, bf16[1024,1024]{1,0:T(8,128)(2,1)}, bf16[1024,1024]{1,0:T(8,128)(2,1)}), (bf16[1024,3,256]{2,0,1:T(8,128)(2,1)}, bf16[1024,1024]{1,0:T(8,128)(2,1)}, bf16[1024,1024]{1,0:T(8,128)(2,1)})) %all-reduce.9.cloned.1.call-update) | async-done | bytes 5767184 | tf_op jit(solution)/shard_map/psum | solution.py:303
  636.6 13.9 %reduce-scatter.14.cloned.1.call-done = bf16[1,32,1024]{2,1,0:T(8,128)(2,1)} async-done(((bf16[4,32,1024]{2,1,0:T(8,128)(2,1)}), bf16[1,32,1024]{2,1,0:T(8,128)(2,1)}) %reduce-scatter.14.cloned.1.call-update) | async-done | bytes 65552 | tf_op jit(solution)/shard_map/reduce_scatter | solution.py:239
  650.4 10.1 %all-gather.2 = bf16[1,256,1024]{2,1,0:T(8,128)(2,1)S(1)} all-gather(bf16[1,32,1024]{2,1,0:T(8,128)(2,1)} %reduce-scatter.14.cloned.1.call-done), channel_id=4, replica_groups=mesh['dp'=8,'mp'=4] {'dp'}, dimensions={1}, use_global_device_ids=true | all-gather | bytes 589824 | tf_op jit(solution)/shard_map/all_gather | solution.py:240
  661.6 32.9 %reduce-scatter.10.cloned.1.call-done = bf16[256,1024]{1,0:T(8,128)(2,1)} async-done(((bf16[1024,1024]{1,0:T(8,128)(2,1)}), bf16[256,1024]{1,0:T(8,128)(2,1)}) %reduce-scatter.10.cloned.1.call-update) | async-done | bytes 524304 | tf_op jit(solution)/shard_map/reduce_scatter | solution.py:295
  701.6 40.7 %all-reduce = (f32[1024]{0:T(1024)S(1)}, f32[1024]{0:T(1024)S(1)}, f32[1024]{0:T(1024)}, f32[1024]{0:T(1024)}, f32[1024]{0:T(1024)}, /*index=5*/f32[1024]{0:T(10...) all-reduce(f32[1024]{0:T(1024)S(1)} %get-tuple-element.176, ...), channel_id=1, replica_groups=mesh['dp'=8,'mp'=4] {'dp','mp'}, use_global_device_ids=true, to_apply=%region_28.29 | all-reduce | flops 9216 | bytes 73728 | tf_op jit(solution)/shard_map/psum | solution.py:309
  (296 shorter events, 182.9 us)
Async XLA Ops:
  7.2 241.0 %copy-start = (bf16[1024,1024]{1,0:T(8,128)(2,1)S(1)}, bf16[1024,1024]{1,0:T(8,128)(2,1)}, u32[]{:S(2)}) copy-start(bf16[1024,1024]{1,0:T(8,128)(2,1)} %param.39) | copy-start | bytes 6291460
  7.2 95.6 %all-gather.8.cloned.1.call-start = ((), (), s32[]{:S(2)}) async-start(), calls=%async_computation.9 | async-start | bytes 2621440 | tf_op jit(solution)/shard_map/all_gather | solution.py:102
  50.7 110.8 %copy-start.30 = (f32[1024]{0:T(1024)}, f32[1024]{0:T(1024)S(1)}, u32[]{:S(2)}) copy-start(f32[1024]{0:T(1024)S(1)} %get-tuple-element.261) | copy-start | bytes 12292
  50.7 110.8 %copy-start.32 = (f32[1024]{0:T(1024)}, f32[1024]{0:T(1024)S(1)}, u32[]{:S(2)}) copy-start(f32[1024]{0:T(1024)S(1)} %get-tuple-element.262) | copy-start | bytes 12292
  55.6 90.8 %all-gather.12.cloned.1.call-start = ((), (), s32[]{:S(2)}) async-start(), calls=%async_computation.17 | async-start | bytes 2359296 | tf_op jit(solution)/shard_map/all_gather | solution.py:47
  138.1 19.0 %all-to-all-start = ((bf16[4,256,256]{1,2,0:T(8,128)(2,1)}), bf16[4,256,256]{1,2,0:T(8,128)(2,1)}, u32[]{:S(2)}, u32[]{:S(2)}) async-start(bf16[4,256,256]{1,2,0:T(8,128)(2,1)} %copy.76), calls=%async_computation | async-start | bytes 1048576 | tf_op jit(solution)/shard_map/all_to_all | solution.py:137
  157.1 13.9 %all-to-all-start.2 = ((bf16[8,64,512]{2,1,0:T(8,128)(2,1)}), bf16[8,64,512]{2,1,0:T(8,128)(2,1)}, u32[]{:S(2)}, u32[]{:S(2)}) async-start(bf16[8,64,512]{2,1,0:T(8,128)(2,1)} %bitcast.170), calls=%async_computation.3 | async-start | bytes 1048576 | tf_op jit(solution)/shard_map/all_to_all | solution.py:177
  161.3 66.9 %all-gather.10.cloned.1.call-start = ((), (), s32[]{:S(2)}) async-start(), calls=%async_computation.11 | async-start | bytes 1310720 | tf_op jit(solution)/shard_map/all_gather | solution.py:200
  165.4 14.3 %collective-permute-start = (bf16[1,256,1024]{2,1,0:T(8,128)(2,1)S(1)}, bf16[1,256,1024]{2,1,0:T(8,128)(2,1)}, u32[]{:S(2)}, u32[]{:S(2)}) collective-permute-start(bf16[1,256,1024]{2,1,0:T(8,128)(2,1)S(1)} %fusion.86), channel_id=1, source_target_pairs={{0,1},{1,0},{2,3},{3,2},{4,5},{5,4},{6,7},{7,6},{8,9},{9,8},{10,11... | collective-permute-start | bytes 1572872 | tf_op jit(solution)/shard_map/ppermute | solution.py:21
  173.7 136.2 %reduce-scatter.8.cloned.1.call-start = ((), (), s32[]{:S(2)}) async-start(), calls=%async_computation.12 | async-start | bytes 2621440 | tf_op jit(solution)/shard_map/reduce_scatter | solution.py:223
  183.4 60.9 %collective-permute-start.1 = (bf16[2,256,1024]{2,1,0:T(8,128)(2,1)}, bf16[2,256,1024]{2,1,0:T(8,128)(2,1)}, u32[]{:S(2)}, u32[]{:S(2)}) collective-permute-start(bf16[2,256,1024]{2,1,0:T(8,128)(2,1)} %pad_maximum_fusion.2), channel_id=1, source_target_pairs={{0,2},{1,3},{2,0},{3,1},{4,6},{5,7},{6,4},{7,5},{8,10},{9,11},{10,... | collective-permute-start | bytes 3145736 | tf_op jit(solution)/shard_map/ppermute | solution.py:21
  267.2 134.1 %reduce-scatter.12.cloned.1.call-start = ((), (), s32[]{:S(2)}) async-start(), calls=%async_computation.14 | async-start | bytes 2359296 | tf_op jit(solution)/shard_map/reduce_scatter | solution.py:238
  320.3 86.5 %reduce-scatter.6.cloned.1.call-start = ((), (), s32[]{:S(2)}) async-start(), calls=%async_computation.10 | async-start | bytes 1310720 | tf_op jit(solution)/shard_map/reduce_scatter | solution.py:148
  340.9 17.9 %all-to-all-start.3 = ((bf16[256,4,256]{2,0,1:T(8,128)(2,1)}), bf16[256,4,256]{2,0,1:T(8,128)(2,1)S(1)}, u32[]{:S(2)}, u32[]{:S(2)}) async-start(bf16[256,4,256]{2,0,1:T(8,128)(2,1)} %bitcast.167), calls=%async_computation.5 | async-start | bytes 1048576 | tf_op jit(solution)/shard_map/all_to_all | solution.py:241
  344.4 181.4 %all-reduce.7.cloned.1.call-start = ((), (), s32[]{:S(2)}) async-start(), calls=%async_computation.16 | async-start | bytes 2097152 | tf_op jit(solution)/shard_map/psum | solution.py:307
  347.5 280.5 %all-reduce.9.cloned.1.call-start = ((), (), s32[]{:S(2)}) async-start(), calls=%async_computation.18 | async-start | bytes 11534336 | tf_op jit(solution)/shard_map/psum | solution.py:303
  401.3 249.2 %reduce-scatter.14.cloned.1.call-start = ((), (), s32[]{:S(2)}) async-start(), calls=%async_computation.15 | async-start | bytes 327680 | tf_op jit(solution)/shard_map/reduce_scatter | solution.py:239
  402.1 292.4 %reduce-scatter.10.cloned.1.call-start = ((), (), s32[]{:S(2)}) async-start(), calls=%async_computation.13 | async-start | bytes 2621440 | tf_op jit(solution)/shard_map/reduce_scatter | solution.py:295
  406.8 121.8 %copy-start.61 = (f32[512]{0:T(512)S(1)}, f32[512]{0:T(512)}, u32[]{:S(2)}) copy-start(f32[512]{0:T(512)} %param.43) | copy-start | bytes 6148
  409.6 119.0 %all-to-all-start.1 = ((bf16[8,64,512]{2,1,0:T(8,128)(2,1)}), bf16[8,64,512]{2,1,0:T(8,128)(2,1)S(1)}, u32[]{:S(2)}, u32[]{:S(2)}) async-start(bf16[8,64,512]{2,1,0:T(8,128)(2,1)} %bitcast.21), calls=%async_computation.2 | async-start | bytes 1048576 | tf_op jit(solution)/shard_map/all_to_all | solution.py:170
  414.8 117.1 %copy-start.53 = (f32[1024]{0:T(1024)S(1)}, f32[1024]{0:T(1024)}, u32[]{:S(2)}) copy-start(f32[1024]{0:T(1024)} %get-tuple-element.237) | copy-start | bytes 12292
  636.6 65.0 %copy-start.41 = (f32[1024]{0:T(1024)S(1)}, f32[1024]{0:T(1024)}, u32[]{:S(2)}) copy-start(f32[1024]{0:T(1024)} %get-tuple-element.177) | copy-start | bytes 12292
  636.6 65.0 %copy-start.42 = (f32[1024]{0:T(1024)S(1)}, f32[1024]{0:T(1024)}, u32[]{:S(2)}) copy-start(f32[1024]{0:T(1024)} %get-tuple-element.240) | copy-start | bytes 12292
  636.6 65.0 %copy-start.55 = (f32[512]{0:T(512)S(1)}, f32[512]{0:T(512)}, u32[]{:S(2)}) copy-start(f32[512]{0:T(512)} %get-tuple-element.257) | copy-start | bytes 6148
  (65 other events, 1005.2 us)
Sparse Core Ops, SparseCore 0:
  55.7 47.0 all-gather.7
  104.6 26.8 all-gather.11
  173.8 54.3 all-gather.9
  267.4 42.4 reduce-scatter.7
  320.4 40.2 reduce-scatter.11
  363.4 27.3 reduce-scatter.5
  396.5 129.1 all-reduce.6
  530.5 97.5 all-reduce.8
  630.3 20.0 reduce-scatter.13
  652.6 41.8 reduce-scatter.9
